TPU v7x, 512 devices: a whole 4x4x16 slice. The times are simulated.
512 devices in a mesh: head: 16 (over y_lo, x, core), gx: 32 (over y_hi, z).
Axes of the slice: x: 4, y: 4 (y_hi: 2, y_lo: 2; y = y_hi * 2 + y_lo), z: 16, core: 2. Of those that a mesh axis runs over, the one named last changes fastest.
Arguments:
- level_set: float32 [288, 192, 8, 128], P('gx', 'head'), may hold values from -6 to 6
- wind_field: float32 [2, 288, 128], P(None, 'gx'), may hold values from -3 to 3
- target_mask: int32 [288, 128], P('gx'), may hold values 0 or 1
- target_depth: float32 [288, 128], P('gx'), may hold values from 0.2 to 2
Outputs:
- level_next: float32 [288, 192, 8, 128], P('gx', 'head')
Inputs may be any that keep to these rules, and one draw needn't show every extreme that they name: `target_mask`: 1 marks a cell of the target set, 0 a cell outside it.
All inputs are finite; a program needn't handle non-finite values. No bound on the sum of `target_mask` on one device may be relied on, other than what follows from the above.
Results may differ from a plain program's by a relative error of at most 0.0003.
Values sent between devices are 32-bit elements; how exact they have to be, the bound alone decides.
A program may use at most 64 MiB of HBM per device.

v0:
```python
import math

import jax
import jax.numpy as jnp
from jax import lax
from jax.sharding import PartitionSpec as P

epsilon = 1e-06
courant = 0.5
spacing = 0.05
turn_limit = 1.0
thrust_limit = 0.5
speed_low = 0.5
speed_high = 1.5


def with_halo(array, sides, width, wrap):
    for axis, dim in sides:
        size, length = (lax.axis_size(axis), array.shape[dim])
        up = [(i, (i + 1) % size) for i in range(size if wrap else size - 1)]
        down = [(j, i) for i, j in up]
        last = lax.slice_in_dim(array, length - width, length, axis=dim)
        leading = lax.slice_in_dim(array, 0, width, axis=dim)
        before = lax.ppermute(last, axis, up)
        after = lax.ppermute(leading, axis, down)
        array = jnp.concatenate([before, array, after], axis=dim)
    return array


def weno_side(slope_a, slope_b, slope_c, slope_d, slope_e):
    guess_a = slope_a / 3.0 - 7.0 * slope_b / 6.0 + 11.0 * slope_c / 6.0
    guess_b = -slope_b / 6.0 + 5.0 * slope_c / 6.0 + slope_d / 3.0
    guess_c = slope_c / 3.0 + 5.0 * slope_d / 6.0 - slope_e / 6.0
    bend_a = slope_a - 2.0 * slope_b + slope_c
    tilt_a = slope_a - 4.0 * slope_b + 3.0 * slope_c
    bend_b = slope_b - 2.0 * slope_c + slope_d
    tilt_b = slope_b - slope_d
    bend_c = slope_c - 2.0 * slope_d + slope_e
    tilt_c = 3.0 * slope_c - 4.0 * slope_d + slope_e
    smooth_a = 13.0 / 12.0 * bend_a * bend_a + 0.25 * tilt_a * tilt_a + epsilon
    smooth_b = 13.0 / 12.0 * bend_b * bend_b + 0.25 * tilt_b * tilt_b + epsilon
    smooth_c = 13.0 / 12.0 * bend_c * bend_c + 0.25 * tilt_c * tilt_c + epsilon
    weight_a = 0.1 / (smooth_a * smooth_a)
    weight_b = 0.6 / (smooth_b * smooth_b)
    weight_c = 0.3 / (smooth_c * smooth_c)
    return (weight_a * guess_a + weight_b * guess_b + weight_c * guess_c) / (
        weight_a + weight_b + weight_c
    )


def weno_pair(padded, along, step_size):
    inner_count = padded.shape[along] - 6
    differences = jnp.diff(padded, axis=along) / step_size

    def window(offset):
        return lax.slice_in_dim(differences, offset, offset + inner_count, axis=along)

    minus_side = weno_side(window(0), window(1), window(2), window(3), window(4))
    plus_side = weno_side(window(5), window(4), window(3), window(2), window(1))
    return (minus_side, plus_side)


def hamilton(
    padded, heading_step, speed_step, speeds, cosines, sines, wind_x, wind_y, peak_x, peak_y
):
    inner = padded[3:-3, 3:-3]
    minus_x, plus_x = weno_pair(padded[:, 3:-3], 0, spacing)
    minus_t, plus_t = weno_pair(padded[3:-3], 1, heading_step)
    minus_v, plus_v = weno_pair(
        jnp.pad(inner, ((0, 0), (0, 0), (3, 3), (0, 0)), mode="edge"), 2, speed_step
    )
    minus_y, plus_y = weno_pair(
        jnp.pad(inner, ((0, 0), (0, 0), (0, 0), (3, 3)), mode="edge"), 3, spacing
    )
    flow_x = speeds * cosines + wind_x
    flow_y = speeds * sines + wind_y
    slope_x = 0.5 * (minus_x + plus_x)
    slope_y = 0.5 * (minus_y + plus_y)
    slope_t = 0.5 * (minus_t + plus_t)
    slope_v = 0.5 * (minus_v + plus_v)
    drift = (
        slope_x * flow_x
        + slope_y * flow_y
        - turn_limit * jnp.abs(slope_t)
        - thrust_limit * jnp.abs(slope_v)
    )
    spread = (
        peak_x * (plus_x - minus_x)
        + peak_y * (plus_y - minus_y)
        + turn_limit * (plus_t - minus_t)
        + thrust_limit * (plus_v - minus_v)
    )
    return drift + 0.5 * spread


def clamp_ends(values, margin):
    position = lax.axis_index("gx")
    last_index = lax.axis_size("gx") - 1
    low_fill = jnp.broadcast_to(values[margin : margin + 1], (margin,) + values.shape[1:])
    high_fill = jnp.broadcast_to(values[-margin - 1 : -margin], (margin,) + values.shape[1:])
    low_part = jnp.where(position == 0, low_fill, values[:margin])
    high_part = jnp.where(position == last_index, high_fill, values[-margin:])
    return jnp.concatenate([low_part, values[margin:-margin], high_part], 0)


def heading_table(first_index, length, heading_total, heading_step):
    indices = jnp.mod(first_index + jnp.arange(length, dtype=jnp.int32), heading_total)
    angles = indices.astype(jnp.float32) * heading_step
    return (jnp.cos(angles).reshape(1, length, 1, 1), jnp.sin(angles).reshape(1, length, 1, 1))


def rimmed(values):
    beside_all = with_halo(values, (("head", 1),), 3, True)
    wide = with_halo(beside_all, (("gx", 0),), 3, False)
    return clamp_ends(wide, 3)


def local(level_set, wind_field, target_mask, target_depth):
    planes, headings, speed_count, cross_count = level_set.shape
    heading_total = headings * lax.axis_size("head")
    heading_step = 2.0 * math.pi / heading_total
    speed_step = (speed_high - speed_low) / (speed_count - 1)
    speed_row = (
        speed_low + jnp.arange(speed_count, dtype=jnp.int32).astype(jnp.float32) * speed_step
    )
    speeds = speed_row.reshape(1, 1, speed_count, 1)
    first_heading = lax.axis_index("head") * headings
    wind_x = wind_field[0]
    wind_y = wind_field[1]
    target_flat = jnp.where(target_mask == 1, -target_depth, target_depth)
    target = target_flat[:, None, None, :]
    local_cos, local_sin = heading_table(first_heading, headings, heading_total, heading_step)
    products_x = local_cos.reshape(headings, 1) * speed_row[None, :]
    products_y = local_sin.reshape(headings, 1) * speed_row[None, :]
    local_x = jnp.max(jnp.abs(products_x[None, :, :, None] + wind_x[:, None, None, :]))
    local_y = jnp.max(jnp.abs(products_y[None, :, :, None] + wind_y[:, None, None, :]))
    peak_x, peak_y = lax.pmax((local_x, local_y), ("head", "gx"))
    time_step = courant / (
        peak_x / spacing + peak_y / spacing + turn_limit / heading_step + thrust_limit / speed_step
    )
    cosines, sines = heading_table(first_heading, headings, heading_total, heading_step)
    flow_wx = wind_x[:, None, None, :]
    flow_wy = wind_y[:, None, None, :]

    def rate_of(values):
        return hamilton(
            rimmed(values),
            heading_step,
            speed_step,
            speeds,
            cosines,
            sines,
            flow_wx,
            flow_wy,
            peak_x,
            peak_y,
        )

    section_one = jnp.minimum(level_set + time_step * rate_of(level_set), target)
    section_two = jnp.minimum(
        0.75 * level_set + 0.25 * (section_one + time_step * rate_of(section_one)), target
    )
    level_next = jnp.minimum(
        1.0 / 3.0 * level_set + 2.0 / 3.0 * (section_two + time_step * rate_of(section_two)), target
    )
    return level_next


def solution(mesh):
    return jax.shard_map(
        local,
        mesh=mesh,
        in_specs=(P("gx", "head", None, None), P(None, "gx", None), P("gx", None), P("gx", None)),
        out_specs=P("gx", "head", None, None),
        check_vma=False,
    )
```

profile of v0, /device:TPU:16, one launch (start us, length us, event | category | flops | bytes accessed | tf_op | source)
XLA Modules:
  0.0 220.1 jit_solution(1420972177609815090)
XLA Ops:
  0.0 1.0 fusion.341
  1.0 4.8 %collective-permute-start.1 = (f32[9,3,8,128]{3,2,1,0:T(8,128)S(1)}, f32[9,3,8,128]{3,2,1,0:T(8,128)S(1)}, u32[]{:S(2)}, u32[]{:S(2)}) collective-permute-start(f32[9,3,8,128]{3,2,1,0:T(8,128)S(1)} %get-tuple-element.33), channel_id=1, source_target_pairs={{32,0},{64,32},{96,64},{128,96},{160,128},{192,160},{224,192},{256... | collective-permute-start | bytes 331784 | tf_op jit(solution)/shard_map/ppermute | solution.py:25
  5.9 1.9 collective-permute-start
  7.8 1.3 fusion.342
  9.1 0.2 fusion.340
  9.8 0.9 copy.164
  10.7 0.9 copy.165
  11.6 0.2 reshape.235
  11.8 0.2 reshape.234
  12.0 0.4 pad_maximum_fusion.3
  12.5 0.3 fusion.5
  12.8 0.7 fusion.326
  13.5 0.8 fusion.300
  14.3 109.5 %all-reduce = (f32[]{:T(128)}, f32[]{:T(128)}) all-reduce(f32[]{:T(128)} %fusion.326, f32[]{:T(128)} %fusion.300), channel_id=1, replica_groups=mesh['head'=16,'gx'=32] {'head','gx'}, use_global_device_ids=true, to_apply=%region_3.4 | all-reduce | flops 2 | bytes 16 | tf_op jit(solution)/shard_map/pmax | solution.py:137
  125.1 0.9 constant_dynamic-update-slice_fusion.2
  126.2 2.9 %collective-permute-start.2 = (f32[3,18,8,128]{3,2,1,0:T(8,128)S(1)}, f32[3,18,8,128]{3,2,1,0:T(8,128)S(1)}, u32[]{:S(2)}, u32[]{:S(2)}) collective-permute-start(f32[3,18,8,128]{3,2,1,0:T(8,128)S(1)} %get-tuple-element.17), channel_id=1, source_target_pairs={{0,1},{1,2},{2,3},{3,4},{4,5},{5,6},{6,7},{7,8},{8,9},{9,10},{10,1... | collective-permute-start | bytes 663560 | tf_op jit(solution)/shard_map/ppermute | solution.py:24
  129.1 6.5 %collective-permute-start.3 = (f32[3,18,8,128]{3,2,1,0:T(8,128)S(1)}, f32[3,18,8,128]{3,2,1,0:T(8,128)S(1)}, u32[]{:S(2)}, u32[]{:S(2)}) collective-permute-start(f32[3,18,8,128]{3,2,1,0:T(8,128)S(1)} %get-tuple-element.18), channel_id=1, source_target_pairs={{1,0},{2,1},{3,2},{4,3},{5,4},{6,5},{7,6},{8,7},{9,8},{10,9},{11,1... | collective-permute-start | bytes 663560 | tf_op jit(solution)/shard_map/ppermute | solution.py:25
  135.7 3.2 %collective-permute-done.2 = f32[3,18,8,128]{3,2,1,0:T(8,128)S(1)} collective-permute-done((f32[3,18,8,128]{3,2,1,0:T(8,128)S(1)}, f32[3,18,8,128]{3,2,1,0:T(8,128)S(1)}, u32[]{:S(2)}, u32[]{:S(2)}) %collective-permute-start.2) | collective-permute-done | bytes 221216 | tf_op jit(solution)/shard_map/ppermute | solution.py:24
  138.9 1.2 collective-permute-done.3
  140.2 9.7 %fusion.307 = f32[9,12,8,128]{3,2,1,0:T(8,128)S(1)} fusion(f32[9,12,8,128]{3,2,1,0:T(8,128)S(1)} %copy-done, f32[9,12,13,128]{3,2,1,0:T(8,128)S(1)} %fusion.4, f32[9,17,8,128]{3,2,1,0:T(8,128)S(1)} %fusion.11, f32[9,12,8,133]{3,2,1,0:T(8,128)S(1)} %fusion.5, f32[14,12,8,128]{3,2,1,0:T(8,128)S(1)} %fusion.8, f32[9,128]{1,0:T(8,128)S(1)} %negate_select_fusion, ...), kind=kLoop, calls=%fused_computation.482 | loop fusion | flops 58503168 | bytes 11516172 | tf_op jit(solution)/shard_map/min | solution.py:159
  150.0 0.2 fusion.337
  150.2 1.9 collective-permute-start.4
  152.2 5.8 %collective-permute-start.5 = (f32[9,3,8,128]{3,2,1,0:T(8,128)S(1)}, f32[9,3,8,128]{3,2,1,0:T(8,128)S(1)}, u32[]{:S(2)}, u32[]{:S(2)}) collective-permute-start(f32[9,3,8,128]{3,2,1,0:T(8,128)S(1)} %get-tuple-element.28), channel_id=1, source_target_pairs={{32,0},{64,32},{96,64},{128,96},{160,128},{192,160},{224,192},{256... | collective-permute-start | bytes 331784 | tf_op jit(solution)/shard_map/ppermute | solution.py:25
  158.3 0.9 copy.150
  159.2 0.9 copy.151
  160.1 0.2 reshape.239
  160.3 0.2 reshape.238
  160.5 0.4 pad_maximum_fusion.5
  160.9 0.3 fusion.3
  161.3 1.9 collective-permute-start.6
  163.3 8.0 %collective-permute-start.7 = (f32[3,18,8,128]{3,2,1,0:T(8,128)S(1)}, f32[3,18,8,128]{3,2,1,0:T(8,128)S(1)}, u32[]{:S(2)}, u32[]{:S(2)}) collective-permute-start(f32[3,18,8,128]{3,2,1,0:T(8,128)S(1)} %get-tuple-element.14), channel_id=1, source_target_pairs={{1,0},{2,1},{3,2},{4,3},{5,4},{6,5},{7,6},{8,7},{9,8},{10,9},{11,1... | collective-permute-start | bytes 663560 | tf_op jit(solution)/shard_map/ppermute | solution.py:25
  171.4 1.9 collective-permute-done.6
  173.3 1.4 collective-permute-done.7
  174.9 9.6 %fusion.316 = f32[9,12,8,128]{3,2,1,0:T(8,128)S(1)} fusion(f32[9,12,8,128]{3,2,1,0:T(8,128)S(1)} %fusion.307, f32[9,12,13,128]{3,2,1,0:T(8,128)S(1)} %fusion.2, f32[9,17,8,128]{3,2,1,0:T(8,128)S(1)} %fusion.10, f32[9,12,8,133]{3,2,1,0:T(8,128)S(1)} %fusion.3, f32[14,12,8,128]{3,2,1,0:T(8,128)S(1)} %fusion.7, f32[9,12,8,128]{3,2,1,0:T(8,128)S(1)} %copy-done, ...), kind=kLoop, calls=%fused_computation.491 | loop fusion | flops 58834944 | bytes 11958540 | tf_op jit(solution)/shard_map/min | solution.py:160
  184.6 0.2 fusion.334
  184.9 1.9 collective-permute-start.8
  186.8 5.9 %collective-permute-start.9 = (f32[9,3,8,128]{3,2,1,0:T(8,128)S(1)}, f32[9,3,8,128]{3,2,1,0:T(8,128)S(1)}, u32[]{:S(2)}, u32[]{:S(2)}) collective-permute-start(f32[9,3,8,128]{3,2,1,0:T(8,128)S(1)} %get-tuple-element.22), channel_id=1, source_target_pairs={{32,0},{64,32},{96,64},{128,96},{160,128},{192,160},{224,192},{256... | collective-permute-start | bytes 331784 | tf_op jit(solution)/shard_map/ppermute | solution.py:25
  193.1 0.9 copy.152
  194.0 0.9 copy.153
  195.0 0.2 reshape.243
  195.2 0.2 reshape.242
  195.3 0.4 pad_maximum_fusion.7
  195.8 0.3 fusion.1
  196.2 1.9 collective-permute-start.10
  198.1 8.0 %collective-permute-start.11 = (f32[3,18,8,128]{3,2,1,0:T(8,128)S(1)}, f32[3,18,8,128]{3,2,1,0:T(8,128)S(1)}, u32[]{:S(2)}, u32[]{:S(2)}) collective-permute-start(f32[3,18,8,128]{3,2,1,0:T(8,128)S(1)} %get-tuple-element.10), channel_id=1, source_target_pairs={{1,0},{2,1},{3,2},{4,3},{5,4},{6,5},{7,6},{8,7},{9,8},{10,9},{11,1... | collective-permute-start | bytes 663560 | tf_op jit(solution)/shard_map/ppermute | solution.py:25
  206.2 1.9 collective-permute-done.10
  208.1 1.4 collective-permute-done.11
  209.7 10.4 %fusion.325 = f32[9,12,8,128]{3,2,1,0:T(8,128)} fusion(f32[9,12,8,128]{3,2,1,0:T(8,128)S(1)} %fusion.316, f32[9,12,13,128]{3,2,1,0:T(8,128)S(1)} %fusion, f32[9,17,8,128]{3,2,1,0:T(8,128)S(1)} %fusion.9, f32[9,12,8,133]{3,2,1,0:T(8,128)S(1)} %fusion.1, f32[14,12,8,128]{3,2,1,0:T(8,128)S(1)} %fusion.6, f32[9,12,8,128]{3,2,1,0:T(8,128)S(1)} %copy-done, ...), kind=kLoop, calls=%fused_computation.500 | loop fusion | flops 58834944 | bytes 11958540 | tf_op jit(solution)/shard_map/min | solution.py:163
  (66 shorter events, 2.5 us)
Async XLA Ops:
  0.0 9.1 %copy-start = (f32[9,12,8,128]{3,2,1,0:T(8,128)S(1)}, f32[9,12,8,128]{3,2,1,0:T(8,128)}, u32[]{:S(2)}) copy-start(f32[9,12,8,128]{3,2,1,0:T(8,128)} %param.4) | copy-start | bytes 1327108
  1.0 8.3 %copy-start.1 = (f32[2,9,128]{2,0,1:T(2,128)S(1)}, f32[2,9,128]{2,0,1:T(2,128)}, u32[]{:S(2)}) copy-start(f32[2,9,128]{2,0,1:T(2,128)} %param.5) | copy-start | bytes 27652
  1.0 125.0 %collective-permute-start.1 = (f32[9,3,8,128]{3,2,1,0:T(8,128)S(1)}, f32[9,3,8,128]{3,2,1,0:T(8,128)S(1)}, u32[]{:S(2)}, u32[]{:S(2)}) collective-permute-start(f32[9,3,8,128]{3,2,1,0:T(8,128)S(1)} %get-tuple-element.33), channel_id=1, source_target_pairs={{32,0},{64,32},{96,64},{128,96},{160,128},{192,160},{224,192},{256... | collective-permute-start | bytes 331784 | tf_op jit(solution)/shard_map/ppermute | solution.py:25
  5.9 119.2 %collective-permute-start = (f32[9,3,8,128]{3,2,1,0:T(8,128)S(1)}, f32[9,3,8,128]{3,2,1,0:T(8,128)}, u32[]{:S(2)}, u32[]{:S(2)}) collective-permute-start(f32[9,3,8,128]{3,2,1,0:T(8,128)S(1)} %get-tuple-element.34), channel_id=1, source_target_pairs={{0,32},{32,64},{64,96},{96,128},{128,160},{160,192},{192,224},{224... | collective-permute-start | bytes 331784 | tf_op jit(solution)/shard_map/ppermute | solution.py:24
  12.4 1.9 copy-start.2
  12.4 1.9 copy-start.3
  126.2 12.7 %collective-permute-start.2 = (f32[3,18,8,128]{3,2,1,0:T(8,128)S(1)}, f32[3,18,8,128]{3,2,1,0:T(8,128)S(1)}, u32[]{:S(2)}, u32[]{:S(2)}) collective-permute-start(f32[3,18,8,128]{3,2,1,0:T(8,128)S(1)} %get-tuple-element.17), channel_id=1, source_target_pairs={{0,1},{1,2},{2,3},{3,4},{4,5},{5,6},{6,7},{7,8},{8,9},{9,10},{10,1... | collective-permute-start | bytes 663560 | tf_op jit(solution)/shard_map/ppermute | solution.py:24
  129.1 10.9 %collective-permute-start.3 = (f32[3,18,8,128]{3,2,1,0:T(8,128)S(1)}, f32[3,18,8,128]{3,2,1,0:T(8,128)S(1)}, u32[]{:S(2)}, u32[]{:S(2)}) collective-permute-start(f32[3,18,8,128]{3,2,1,0:T(8,128)S(1)} %get-tuple-element.18), channel_id=1, source_target_pairs={{1,0},{2,1},{3,2},{4,3},{5,4},{6,5},{7,6},{8,7},{9,8},{10,9},{11,1... | collective-permute-start | bytes 663560 | tf_op jit(solution)/shard_map/ppermute | solution.py:25
  150.2 11.0 %collective-permute-start.4 = (f32[9,3,8,128]{3,2,1,0:T(8,128)S(1)}, f32[9,3,8,128]{3,2,1,0:T(8,128)S(1)}, u32[]{:S(2)}, u32[]{:S(2)}) collective-permute-start(f32[9,3,8,128]{3,2,1,0:T(8,128)S(1)} %get-tuple-element.27), channel_id=1, source_target_pairs={{0,32},{32,64},{64,96},{96,128},{128,160},{160,192},{192,224},{224... | collective-permute-start | bytes 331784 | tf_op jit(solution)/shard_map/ppermute | solution.py:24
  152.2 9.1 %collective-permute-start.5 = (f32[9,3,8,128]{3,2,1,0:T(8,128)S(1)}, f32[9,3,8,128]{3,2,1,0:T(8,128)S(1)}, u32[]{:S(2)}, u32[]{:S(2)}) collective-permute-start(f32[9,3,8,128]{3,2,1,0:T(8,128)S(1)} %get-tuple-element.28), channel_id=1, source_target_pairs={{32,0},{64,32},{96,64},{128,96},{160,128},{192,160},{224,192},{256... | collective-permute-start | bytes 331784 | tf_op jit(solution)/shard_map/ppermute | solution.py:25
  161.3 11.9 %collective-permute-start.6 = (f32[3,18,8,128]{3,2,1,0:T(8,128)S(1)}, f32[3,18,8,128]{3,2,1,0:T(8,128)S(1)}, u32[]{:S(2)}, u32[]{:S(2)}) collective-permute-start(f32[3,18,8,128]{3,2,1,0:T(8,128)S(1)} %get-tuple-element.13), channel_id=1, source_target_pairs={{0,1},{1,2},{2,3},{3,4},{4,5},{5,6},{6,7},{7,8},{8,9},{9,10},{10,1... | collective-permute-start | bytes 663560 | tf_op jit(solution)/shard_map/ppermute | solution.py:24
  163.3 11.4 %collective-permute-start.7 = (f32[3,18,8,128]{3,2,1,0:T(8,128)S(1)}, f32[3,18,8,128]{3,2,1,0:T(8,128)S(1)}, u32[]{:S(2)}, u32[]{:S(2)}) collective-permute-start(f32[3,18,8,128]{3,2,1,0:T(8,128)S(1)} %get-tuple-element.14), channel_id=1, source_target_pairs={{1,0},{2,1},{3,2},{4,3},{5,4},{6,5},{7,6},{8,7},{9,8},{10,9},{11,1... | collective-permute-start | bytes 663560 | tf_op jit(solution)/shard_map/ppermute | solution.py:25
  184.9 11.2 %collective-permute-start.8 = (f32[9,3,8,128]{3,2,1,0:T(8,128)S(1)}, f32[9,3,8,128]{3,2,1,0:T(8,128)S(1)}, u32[]{:S(2)}, u32[]{:S(2)}) collective-permute-start(f32[9,3,8,128]{3,2,1,0:T(8,128)S(1)} %get-tuple-element.21), channel_id=1, source_target_pairs={{0,32},{32,64},{64,96},{96,128},{128,160},{160,192},{192,224},{224... | collective-permute-start | bytes 331784 | tf_op jit(solution)/shard_map/ppermute | solution.py:24
  186.8 9.3 %collective-permute-start.9 = (f32[9,3,8,128]{3,2,1,0:T(8,128)S(1)}, f32[9,3,8,128]{3,2,1,0:T(8,128)S(1)}, u32[]{:S(2)}, u32[]{:S(2)}) collective-permute-start(f32[9,3,8,128]{3,2,1,0:T(8,128)S(1)} %get-tuple-element.22), channel_id=1, source_target_pairs={{32,0},{64,32},{96,64},{128,96},{160,128},{192,160},{224,192},{256... | collective-permute-start | bytes 331784 | tf_op jit(solution)/shard_map/ppermute | solution.py:25
  196.2 11.9 %collective-permute-start.10 = (f32[3,18,8,128]{3,2,1,0:T(8,128)S(1)}, f32[3,18,8,128]{3,2,1,0:T(8,128)S(1)}, u32[]{:S(2)}, u32[]{:S(2)}) collective-permute-start(f32[3,18,8,128]{3,2,1,0:T(8,128)S(1)} %get-tuple-element.9), channel_id=1, source_target_pairs={{0,1},{1,2},{2,3},{3,4},{4,5},{5,6},{6,7},{7,8},{8,9},{9,10},{10,1... | collective-permute-start | bytes 663560 | tf_op jit(solution)/shard_map/ppermute | solution.py:24
  198.1 11.4 %collective-permute-start.11 = (f32[3,18,8,128]{3,2,1,0:T(8,128)S(1)}, f32[3,18,8,128]{3,2,1,0:T(8,128)S(1)}, u32[]{:S(2)}, u32[]{:S(2)}) collective-permute-start(f32[3,18,8,128]{3,2,1,0:T(8,128)S(1)} %get-tuple-element.10), channel_id=1, source_target_pairs={{1,0},{2,1},{3,2},{4,3},{5,4},{6,5},{7,6},{8,7},{9,8},{10,9},{11,1... | collective-permute-start | bytes 663560 | tf_op jit(solution)/shard_map/ppermute | solution.py:25
where the time goes:
time: 221 us; the launch traced here: 220 us
  blocking collectives  110 us (50%)
  starting transfers between devices  51.6 us (23%)
  other arithmetic  35.1 us (16%)
  local copies, waits for them, and re-layouts  11 us (5%)
  waiting for transfers between devices  11 us (5%)
    pmax x1, blocking collectives, local(): peak_x, peak_y = lax.pmax((local_x, local_y), ('head', 'gx'))  110 us
    ppermute x6, starting transfers between devices, with_halo(): after = lax.ppermute(leading, axis, down)  39.1 us
    ppermute x6, starting transfers between devices, with_halo(): before = lax.ppermute(last, axis, up)  12.5 us
    min x1, other arithmetic, local(): jnp.minimum(1.0 / 3.0 * level_set + 2.0 / 3.0 * (section_two + time_step...  10.4 us
    min x1, other arithmetic, local(): jnp.minimum(level_set + time_step * rate_of(level_set), target)  9.67 us
    min x1, other arithmetic, local(): jnp.minimum(0.75 * level_set + 0.25 * (section_one + time_step * rate_of(...  9.64 us
    ppermute x6, waiting for transfers between devices, with_halo(): before = lax.ppermute(last, axis, up)  6.96 us
    slice x9, local copies, waits for them, and re-layouts, hamilton(): jnp.pad(inner, ((0, 0), (0, 0), (0, 0), (3, 3)), mode='edge')  6.02 us
  transfers between devices with their start and end apart: 12, of which 6 were waited for; matrix products, arithmetic and copies ran while one was open for 6% of the time, Pallas kernels for 0%

commit v1 on v0

v1 whole, which is shorter than its diff:
```python
import functools
import math

import jax
import jax.numpy as jnp
import numpy as np
from jax import lax
from jax.experimental import pallas as pl
from jax.experimental.pallas import tpu as pltpu
from jax.sharding import PartitionSpec as P

MESH = pl.DeviceIdType.MESH
epsilon = 1e-06
courant = 0.5
spacing = 0.05
turn_limit = 1.0
thrust_limit = 0.5
speed_low = 0.5
speed_high = 1.5
NV = 8
NY = 128
NX = 288
NTH = 192
NXL = 9
NHL = 12
HT = 2.0 * math.pi / NTH
HV = (speed_high - speed_low) / (NV - 1)
EPS_X = 0.75 * epsilon * spacing**2
EPS_T = 0.75 * epsilon * HT**2
EPS_V = 0.75 * epsilon * HV**2
K_T = turn_limit * spacing / HT
K_V = thrust_limit * spacing / HV
Z = 16
NEAR = (-3, -2, -1, 1, 2)
FAR = (-5, 5)


def face(p, q, hp, hq, eps, left, mid, right):
    b = q - p
    b2 = b + b
    smooth = (b * b + eps) + hp * q
    out = {"b2": b2}
    if left:
        s = smooth + hq * b2
        out["L"] = 1.0 / (s * s)
        out["aL"] = out["L"] * (1.0 / 3.0)
    if mid:
        out["M"] = 2.0 / (smooth * smooth)
    if right:
        s = smooth - hp * b2
        out["R"] = 1.0 / (s * s)
        out["aR"] = out["R"] * (1.0 / 3.0)
    return out


def join(a_lo, m_lo, c_lo, k_lo, a_hi, m_hi, c_hi, k_hi, c):
    low = (a_lo * k_lo + c_lo * c) / ((a_lo + c_lo) + m_lo)
    high = (a_hi * k_hi + c_hi * c) / ((a_hi + c_hi) + m_hi)
    return high - low, (high + low) - c


def line(load, n, eps):
    u = {i: load(i) for i in range(-3, n + 3)}
    d = {i: u[i + 1] - u[i] for i in range(-3, n + 2)}
    e = {i: d[i] - d[i - 1] for i in range(-2, n + 2)}
    h = {i: 0.75 * e[i] for i in e}
    f = {
        i: face(e[i], e[i + 1], h[i], h[i + 1], eps, i <= n - 2, -1 <= i <= n - 1, i >= 0)
        for i in range(-2, n + 1)
    }
    k = {i: f[i]["b2"] - f[i - 1]["b2"] for i in range(-1, n + 1)}
    g = {i: 6.0 * u[i] - e[i] for i in range(-1, n + 1)}
    result = []
    for i in range(n):
        diff, jump = join(
            f[i - 2]["aL"], f[i - 1]["M"], f[i]["R"], k[i - 1],
            f[i + 1]["aR"], f[i]["M"], f[i - 1]["L"], k[i + 1],
            0.5 * k[i],
        )
        result.append(((g[i + 1] - g[i - 1]) + diff, jump))
    return result


def along(u, axis, eps, first, last):
    n = u.shape[axis]
    back = lambda a: pltpu.roll(a, 1, axis)
    ahead = lambda a: pltpu.roll(a, n - 1, axis)
    d_lo = u - jnp.where(first, u, back(u))
    d_hi = jnp.where(last, u, ahead(u)) - u
    e = d_hi - d_lo
    b_lo = e - jnp.where(first, 0.0, back(e))
    b_hi = jnp.where(last, 0.0, ahead(e)) - e
    p, q = e - b_lo, b_hi + e
    h = 0.75 * e
    m_lo = (b_lo * b_lo + eps) + h * p
    m_hi = (b_hi * b_hi + eps) + h * q
    s_lo = m_lo + h * (b_lo + b_lo)
    s_hi = m_hi - h * (b_hi + b_hi)
    c_hi = 1.0 / (s_lo * s_lo)
    c_lo = 1.0 / (s_hi * s_hi)
    c = b_hi - b_lo
    k = c + c
    e2 = e + e
    flat = 1.0 / (3.0 * eps * eps)
    a_lo = jnp.where(first, flat, back(c_hi * (1.0 / 3.0)))
    a_hi = jnp.where(last, flat, ahead(c_lo * (1.0 / 3.0)))
    k_lo = jnp.where(first, e2, back(k))
    k_hi = jnp.where(last, e2, ahead(k))
    diff, jump = join(a_lo, 2.0 / (m_lo * m_lo), c_lo, k_lo, a_hi, 2.0 / (m_hi * m_hi), c_hi, k_hi, c)
    return (6.0 * (d_hi + d_lo) - (b_hi + b_lo)) + diff, jump


def iotas():
    shape = (NV, NY)
    row = lax.broadcasted_iota(jnp.int32, shape, 0)
    lane = lax.broadcasted_iota(jnp.int32, shape, 1)
    return row, lane


def speeds_of(row):
    return speed_low + row.astype(jnp.float32) * np.float32(HV)


def pass_vy(u_ref, r_ref, wy_ref, tab_ref, by_ref, pk_ref, lo, hi):
    def body(x, carry):
        row, lane = iotas()
        speeds = speeds_of(row)
        v0, v1 = row == 0, row == NV - 1
        y0, y1 = lane == 0, lane == NY - 1
        wind = wy_ref[x]
        for h in range(NHL):
            u = u_ref[x + 3, h + 3]
            total_v, jump_v = along(u, 0, EPS_V, v0, v1)
            total_y, jump_y = along(u, 1, EPS_X, y0, y1)
            flow = speeds * tab_ref[NHL + h : NHL + h + 1, :] + wind
            rate = total_y * flow + K_V * (jump_v - jnp.abs(total_v))
            if by_ref is not None:
                by_ref[x, h] = jump_y
            else:
                rate = rate + pk_ref[1] * jump_y
            r_ref[x, h] = rate
        return carry

    lax.fori_loop(lo, hi, body, 0)


def pass_h(u_ref, r_ref, lo, hi):
    def body(x, carry):
        for h, (total, jump) in enumerate(line(lambda i: u_ref[x + 3, i + 3], NHL, EPS_T)):
            r_ref[x, h] = r_ref[x, h] + K_T * (jump - jnp.abs(total))
        return carry

    lax.fori_loop(lo, hi, body, 0)


def pass_x(u_ref, wx_ref, tab_ref, lo, finish, group=4):
    def body(t, carry):
        row, _ = iotas()
        speeds = speeds_of(row)
        for j in range(group):
            h = t * group + j
            lanes = speeds * tab_ref[pl.ds(h, 1), :]
            cells = line(lambda i: u_ref[lo + i + 3, h + 3], 3, EPS_X)
            for i, (total, jump) in enumerate(cells):
                finish(lo + i, h, total * (lanes + wx_ref[lo + i]), jump)
        return carry

    lax.fori_loop(0, NHL // group, body, 0)


def bounds():
    speeds = np.float32(speed_low) + np.arange(NV, dtype=np.float32) * np.float32(HV)
    angles = np.arange(NTH, dtype=np.float32) * np.float32(HT)
    px = np.cos(angles)[:, None] * speeds
    py = np.sin(angles)[:, None] * speeds
    return [float(a) for a in (px.max(), -px.min(), py.max(), -py.min())]


def table():
    angles = np.arange(NTH, dtype=np.float32) * np.float32(HT)
    both = np.stack([np.cos(angles).reshape(-1, NHL), np.sin(angles).reshape(-1, NHL)], 1)
    both = both.reshape(NTH // NHL, 2 * NHL, 1).astype(np.float32)
    return np.broadcast_to(both, (NTH // NHL, 2 * NHL, NY)).copy()


def kernel(
    level, wind, mask, depth, tab_all, out,
    u0, u1, u2, r, bx, by, res, wv, mv, dv, tab, wx, wy, tg, pk, pbuf, pmine,
    sem_in, sx, rx, sh, rh, sp, rp, so,
):
    g = lax.axis_index("gx")
    hd = lax.axis_index("head")
    ng, nh = lax.axis_size("gx"), lax.axis_size("head")
    yh, z = g // Z, g % Z
    ring = lambda o: yh * Z + (z + Z + o) % Z
    fields = (u0, u1, u2)

    barrier = pltpu.get_barrier_semaphore()
    peers = [
        {"gx": (g + 1) % ng, "head": hd},
        {"gx": (g + ng - 1) % ng, "head": hd},
        {"gx": g, "head": (hd + 1) % nh},
        {"gx": g, "head": (hd + nh - 1) % nh},
        {"gx": (g + Z) % ng, "head": (hd + nh // 2) % nh},
    ] + [{"gx": ring(o), "head": hd} for o in (-3, -2, -1, 1, 2, 3)]
    for peer in peers:
        pl.semaphore_signal(barrier, inc=1, device_id=peer, device_id_type=MESH)

    get_wind = pltpu.make_async_copy(wind, wv, sem_in.at[0])
    get_wind.start()
    get_level = pltpu.make_async_copy(level, u0.at[pl.ds(3, NXL), pl.ds(3, NHL)], sem_in.at[1])
    get_level.start()
    get_tab = pltpu.make_async_copy(tab_all.at[hd], tab, sem_in.at[2])
    get_tab.start()
    get_mask = pltpu.make_async_copy(mask, mv, sem_in.at[3])
    get_mask.start()
    get_depth = pltpu.make_async_copy(depth, dv, sem_in.at[4])
    get_depth.start()

    get_wind.wait()
    for i in range(NXL):
        wx[i] = jnp.broadcast_to(wv[0, i : i + 1, :], (NV, NY))
        wy[i] = jnp.broadcast_to(wv[1, i : i + 1, :], (NV, NY))
    tops = []
    for c in range(2):
        top, low = wv[c, 0:1, :], wv[c, 0:1, :]
        for i in range(1, NXL):
            top, low = jnp.maximum(top, wv[c, i : i + 1, :]), jnp.minimum(low, wv[c, i : i + 1, :])
        tops += [top, -low]
    row, _ = iotas()
    tile = jnp.broadcast_to(tops[0], (NV, NY))
    for i in range(1, 4):
        tile = jnp.where(row == i, jnp.broadcast_to(tops[i], (NV, NY)), tile)
    for shift in (1, 2, 4, 8, 16, 32, 64):
        tile = jnp.maximum(tile, pltpu.roll(tile, shift, 1))
    pmine[0] = tile

    def x_copy(s, up):
        src = level if s == 0 else fields[s]
        base = 0 if s == 0 else 3
        start = (NXL - 3 if up else 0) + base
        return pltpu.make_async_remote_copy(
            src_ref=src.at[pl.ds(start, 3), pl.ds(base, NHL)],
            dst_ref=fields[s].at[pl.ds(0 if up else NXL + 3, 3), pl.ds(3, NHL)],
            send_sem=sx.at[s, int(up)],
            recv_sem=rx.at[s, int(up)],
            device_id={"gx": (g + 1) % ng if up else (g + ng - 1) % ng, "head": hd},
            device_id_type=MESH,
        )

    def h_copy(s, up, chunk):
        src = level if s == 0 else fields[s]
        base = 0 if s == 0 else 3
        start = (NHL - 3 if up else 0) + base
        return pltpu.make_async_remote_copy(
            src_ref=src.at[pl.ds(3 * chunk + base, 3), pl.ds(start, 3)],
            dst_ref=fields[s].at[pl.ds(3 * chunk + 3, 3), pl.ds(0 if up else NHL + 3, 3)],
            send_sem=sh.at[s, int(up), chunk],
            recv_sem=rh.at[s, int(up), chunk],
            device_id={"gx": g, "head": (hd + 1) % nh if up else (hd + nh - 1) % nh},
            device_id_type=MESH,
        )

    def send_x(s, up):
        @pl.when(g < ng - 1 if up else g > 0)
        def _():
            x_copy(s, up).start()

    def take_x(s, up):
        @pl.when(g > 0 if up else g < ng - 1)
        def _():
            x_copy(s, up).wait_recv()

        @pl.when(g == 0 if up else g == ng - 1)
        def _():
            for h in range(NHL):
                edge = fields[s][3 if up else NXL + 2, h + 3]
                for i in range(3):
                    fields[s][i if up else NXL + 3 + i, h + 3] = edge

    def send_h(s, chunk):
        for up in (True, False):
            h_copy(s, up, chunk).start()

    def take_h(s, chunk):
        for up in (True, False):
            h_copy(s, up, chunk).wait_recv()

    def p_copy(slot, src, dst, to):
        return pltpu.make_async_remote_copy(
            src_ref=pmine.at[src], dst_ref=pbuf.at[dst], send_sem=sp.at[slot], recv_sem=rp.at[slot],
            device_id=to, device_id_type=MESH,
        )

    p_first = [p_copy(0, 0, 0, peers[4])]
    p_near = [p_copy(1 + j, 1, 1 + j, {"gx": ring(o), "head": hd}) for j, o in enumerate(NEAR)]
    p_far = [p_copy(6 + j, 2, 6 + j, {"gx": ring(o), "head": hd}) for j, o in enumerate(FAR)]

    def fold(copies, src, dst):
        best = pmine[src]
        for c in copies:
            c.wait_recv()
        first = {1: 0, 2: 1, 3: 6}[dst]
        for j in range(len(copies)):
            best = jnp.maximum(best, pbuf[first + j])
        pmine[dst] = best

    pl.semaphore_wait(barrier, len(peers))
    for c in p_first:
        c.start()
    send_x(0, True)
    send_x(0, False)
    for chunk in range(3):
        send_h(0, chunk)

    get_mask.wait()
    get_depth.wait()
    for i in range(NXL):
        d = dv[i : i + 1, :]
        tg[i] = jnp.broadcast_to(jnp.where(mv[i : i + 1, :] == 1, -d, d), (NV, NY))
    get_tab.wait()
    get_level.wait()

    pass_vy(u0, r, wy, tab, by, None, 0, 3)
    fold(p_first, 0, 1)
    for c in p_near:
        c.start()
    pass_vy(u0, r, wy, tab, by, None, 3, NXL)
    for chunk in range(3):
        take_h(0, chunk)
    pass_h(u0, r, 0, NXL)
    fold(p_near, 1, 2)
    for c in p_far:
        c.start()

    def keep(x, h, part, jump):
        r[x, h] = r[x, h] + part
        bx[x, h] = jump

    pass_x(u0, wx, tab, 3, keep)
    take_x(0, True)
    pass_x(u0, wx, tab, 0, keep)
    take_x(0, False)
    pass_x(u0, wx, tab, 6, keep)

    fold(p_far, 2, 3)
    top = pmine[3]
    cx, cnx, cy, cny = bounds()
    peak_x = jnp.maximum(top[0:1] + cx, top[1:2] + cnx)
    peak_y = jnp.maximum(top[2:3] + cy, top[3:4] + cny)
    step = courant / (peak_x / spacing + peak_y / spacing + turn_limit / HT + thrust_limit / HV)
    pk[0] = jnp.broadcast_to(peak_x, (NV, NY))
    pk[1] = jnp.broadcast_to(peak_y, (NV, NY))
    pk[2] = jnp.broadcast_to(step * (1.0 / (12.0 * spacing)), (NV, NY))

    def update_one(lo):
        def body(h, carry):
            px, py, dt = pk[0], pk[1], pk[2]
            for i in range(3):
                rate = r[lo + i, h] + px * bx[lo + i, h] + py * by[lo + i, h]
                u1[lo + i + 3, h + 3] = jnp.minimum(u0[lo + i + 3, h + 3] + dt * rate, tg[lo + i])
            return carry

        lax.fori_loop(0, NHL, body, 0, unroll=2)

    update_one(0)
    send_x(1, False)
    send_h(1, 0)
    update_one(6)
    send_x(1, True)
    send_h(1, 2)
    update_one(3)
    send_h(1, 1)

    def section(s, write, after):
        u = fields[s]
        old, new = (0.75, 0.25) if s == 1 else (1.0 / 3.0, 2.0 / 3.0)
        pass_vy(u, r, wy, tab, None, pk, 0, NXL)
        for chunk in (0, 2, 1):
            take_h(s, chunk)
            pass_h(u, r, 3 * chunk, 3 * chunk + 3)

        def finish(x, h, part, jump):
            rate = (r[x, h] + part) + pk[0] * jump
            now = old * u0[x + 3, h + 3] + new * (u[x + 3, h + 3] + pk[2] * rate)
            write(x, h, jnp.minimum(now, tg[x]))

        pass_x(u, wx, tab, 3, finish)
        after(1)
        take_x(s, True)
        pass_x(u, wx, tab, 0, finish)
        after(0)
        take_x(s, False)
        pass_x(u, wx, tab, 6, finish)
        after(2)

    def write_two(x, h, value):
        u2[x + 3, h + 3] = value

    def after_two(chunk):
        if chunk != 1:
            send_x(2, chunk == 2)
        send_h(2, chunk)

    section(1, write_two, after_two)

    def write_out(x, h, value):
        res[x, h] = value

    puts = [
        pltpu.make_async_copy(res.at[pl.ds(3 * c, 3)], out.at[pl.ds(3 * c, 3)], so.at[c]) for c in range(3)
    ]
    section(2, write_out, lambda chunk: puts[chunk].start())

    for put in puts:
        put.wait()
    for c in p_first + p_near + p_far:
        c.wait_send()
    for s in range(3):
        for up in (True, False):

            @pl.when(g < ng - 1 if up else g > 0)
            def _():
                x_copy(s, up).wait_send()

            for chunk in range(3):
                h_copy(s, up, chunk).wait_send()


def local(level_set, wind_field, target_mask, target_depth):
    field = pltpu.VMEM((NXL + 6, NHL + 6, NV, NY), jnp.float32)
    inner = pltpu.VMEM((NXL, NHL, NV, NY), jnp.float32)
    rows = pltpu.VMEM((NXL, NV, NY), jnp.float32)
    dma = pltpu.SemaphoreType.DMA
    return pl.pallas_call(
        kernel,
        out_shape=jax.ShapeDtypeStruct(level_set.shape, jnp.float32),
        in_specs=[pl.BlockSpec(memory_space=pl.ANY)] * 5,
        out_specs=pl.BlockSpec(memory_space=pl.ANY),
        scratch_shapes=[
            field, field, field, inner, inner, inner, inner,
            pltpu.VMEM((2, NXL, NY), jnp.float32),
            pltpu.VMEM((NXL, NY), jnp.int32),
            pltpu.VMEM((NXL, NY), jnp.float32),
            pltpu.VMEM((2 * NHL, NY), jnp.float32),
            rows, rows, rows,
            pltpu.VMEM((3, NV, NY), jnp.float32),
            pltpu.VMEM((8, NV, NY), jnp.float32),
            pltpu.VMEM((4, NV, NY), jnp.float32),
            dma((5,)), dma((3, 2)), dma((3, 2)), dma((3, 2, 3)), dma((3, 2, 3)), dma((8,)), dma((8,)), dma((3,)),
        ],
        compiler_params=pltpu.CompilerParams(collective_id=0, has_side_effects=True),
        name="step",
    )(level_set, wind_field, target_mask, target_depth, jnp.asarray(table()))


def solution(mesh):
    return jax.shard_map(
        local,
        mesh=mesh,
        in_specs=(P("gx", "head", None, None), P(None, "gx", None), P("gx", None), P("gx", None)),
        out_specs=P("gx", "head", None, None),
        check_vma=False,
    )
```

time: 221 us -> 43.4 us (0.20)
  blocking collectives: 110 us -> 0 us
  starting transfers between devices: 51.6 us -> 0 us
  Pallas kernels: 0 us -> 40.1 us
  other arithmetic: 35.1 us -> 0 us
  waiting for transfers between devices: 11 us -> 0 us
  local copies, waits for them, and re-layouts: 11 us -> 3.11 us
    pmax x1 -> x0, blocking collectives: 110 us -> none  [local(): peak_x, peak_y = lax.pmax((local_x, local_y), ('head', 'gx'))]
    ppermute x12 -> x0, starting transfers between devices: 51.6 us -> none  [the longest x6 39.1 us: with_halo(): after = lax.ppermute(leading, axis, down)]
    pallas_call x0 -> x1, Pallas kernels: none -> 40.1 us  [local(): pl.pallas_call(kernel, out_shape=jax.ShapeDtypeStruct(level_set.shape, jn...]
    min x3 -> x0, other arithmetic: 29.7 us -> none  [the longest x1 10.4 us: local(): jnp.minimum(1.0 / 3.0 * level_set + 2.0 / 3.0 * (section_two + time_step...]
    ppermute x12 -> x0, waiting for transfers between devices: 11 us -> none  [the longest x6 6.96 us: with_halo(): before = lax.ppermute(last, axis, up)]
    slice x20 -> x0, local copies, waits for them, and re-layouts: 8.61 us -> none  [the longest x9 6.02 us: hamilton(): jnp.pad(inner, ((0, 0), (0, 0), (0, 0), (3, 3)), mode='edge')]
  transfers between devices with their start and end apart: 12 -> 0, of which waited for: 6 -> 0; matrix products, arithmetic and copies ran while one was open for 6% -> 0% of each run, Pallas kernels for 0% -> 0%
where the time goes in v1:
time: 43.4 us; the launch traced here: 43.2 us
  Pallas kernels  40.1 us (92%)
  local copies, waits for them, and re-layouts  3.11 us (7%)
    pallas_call x1, Pallas kernels, local(): pl.pallas_call(kernel, out_shape=jax.ShapeDtypeStruct(level_set.shape, jn...  40.1 us
    unnamed x2, local copies, waits for them, and re-layouts  3.11 us

profile of v1, /device:TPU:16, one launch (start us, length us, event | category | flops | bytes accessed | tf_op | source)
XLA Modules:
  0.0 43.2 jit_solution(16623374335661969613)
XLA Ops:
  0.0 1.3 %copy.6.wind = f32[2,9,128]{2,1,0:T(8,128)} copy(f32[2,9,128]{2,0,1:T(2,128)} %param.6) | data formatting | bytes 18432 | tf_op args[1]
  1.3 40.1 %step.1 = f32[9,12,8,128]{3,2,1,0:T(8,128)} custom-call(f32[9,12,8,128]{3,2,1,0:T(8,128)} %level.1, f32[2,9,128]{2,1,0:T(8,128)} %copy.6.wind, s32[9,128]{1,0:T(8,128)} %mask.1, f32[9,128]{1,0:T(8,128)} %depth.1, f32[16,24,128]{2,1,0:T(8,128)} %constant.2.clone.tab_all), custom_call_target="tpu_custom_call" | custom-call | tf_op jit(solution)/shard_map/step/pallas_call | solution.py:435
  41.4 1.8 %copy.8 = f32[9,12,8,128]{3,2,1,0:T(8,128)} copy(f32[9,12,8,128]{3,2,1,0:T(8,128)} %step.1) | data formatting | bytes 884736

commit v2 on v1

--- a/solution.py
+++ b/solution.py
@@ -31,8 +31,6 @@
 K_T = turn_limit * spacing / HT
 K_V = thrust_limit * spacing / HV
 Z = 16
-NEAR = (-3, -2, -1, 1, 2)
-FAR = (-5, 5)
 
 
 def face(p, q, hp, hq, eps, left, mid, right):
@@ -192,19 +190,32 @@
     hd = lax.axis_index("head")
     ng, nh = lax.axis_size("gx"), lax.axis_size("head")
     yh, z = g // Z, g % Z
-    ring = lambda o: yh * Z + (z + Z + o) % Z
+    at = lambda half, z_: half * Z + z_
+    across = (hd + nh // 2) % nh
     fields = (u0, u1, u2)
 
     barrier = pltpu.get_barrier_semaphore()
-    peers = [
-        {"gx": (g + 1) % ng, "head": hd},
-        {"gx": (g + ng - 1) % ng, "head": hd},
-        {"gx": g, "head": (hd + 1) % nh},
-        {"gx": g, "head": (hd + nh - 1) % nh},
-        {"gx": (g + Z) % ng, "head": (hd + nh // 2) % nh},
-    ] + [{"gx": ring(o), "head": hd} for o in (-3, -2, -1, 1, 2, 3)]
-    for peer in peers:
+
+    def greet(peer):
         pl.semaphore_signal(barrier, inc=1, device_id=peer, device_id_type=MESH)
+
+    greet({"gx": g, "head": (hd + 1) % nh})
+    greet({"gx": g, "head": (hd + nh - 1) % nh})
+
+    @pl.when(g < ng - 1)
+    def _():
+        greet({"gx": (g + 1) % ng, "head": hd})
+
+    @pl.when(g > 0)
+    def _():
+        greet({"gx": (g + ng - 1) % ng, "head": hd})
+
+    @pl.when(z == 0)
+    def _():
+        for i in range(1, Z):
+            greet({"gx": at(yh, i), "head": hd})
+        for i in range(Z):
+            greet({"gx": at(1 - yh, i), "head": across})
 
     get_wind = pltpu.make_async_copy(wind, wv, sem_in.at[0])
     get_wind.start()
@@ -218,22 +229,17 @@
     get_depth.start()
 
     get_wind.wait()
-    for i in range(NXL):
-        wx[i] = jnp.broadcast_to(wv[0, i : i + 1, :], (NV, NY))
-        wy[i] = jnp.broadcast_to(wv[1, i : i + 1, :], (NV, NY))
     tops = []
     for c in range(2):
-        top, low = wv[c, 0:1, :], wv[c, 0:1, :]
+        top, low = wv[0, c : c + 1, :], wv[0, c : c + 1, :]
         for i in range(1, NXL):
-            top, low = jnp.maximum(top, wv[c, i : i + 1, :]), jnp.minimum(low, wv[c, i : i + 1, :])
+            top, low = jnp.maximum(top, wv[i, c : c + 1, :]), jnp.minimum(low, wv[i, c : c + 1, :])
         tops += [top, -low]
     row, _ = iotas()
     tile = jnp.broadcast_to(tops[0], (NV, NY))
     for i in range(1, 4):
         tile = jnp.where(row == i, jnp.broadcast_to(tops[i], (NV, NY)), tile)
-    for shift in (1, 2, 4, 8, 16, 32, 64):
-        tile = jnp.maximum(tile, pltpu.roll(tile, shift, 1))
-    pmine[0] = tile
+    pmine[0] = jnp.broadcast_to(jnp.max(tile, axis=1, keepdims=True), (NV, NY))
 
     def x_copy(s, up):
         src = level if s == 0 else fields[s]
@@ -286,33 +292,39 @@
         for up in (True, False):
             h_copy(s, up, chunk).wait_recv()
 
-    def p_copy(slot, src, dst, to):
-        return pltpu.make_async_remote_copy(
-            src_ref=pmine.at[src], dst_ref=pbuf.at[dst], send_sem=sp.at[slot], recv_sem=rp.at[slot],
-            device_id=to, device_id_type=MESH,
-        )
-
-    p_first = [p_copy(0, 0, 0, peers[4])]
-    p_near = [p_copy(1 + j, 1, 1 + j, {"gx": ring(o), "head": hd}) for j, o in enumerate(NEAR)]
-    p_far = [p_copy(6 + j, 2, 6 + j, {"gx": ring(o), "head": hd}) for j, o in enumerate(FAR)]
-
-    def fold(copies, src, dst):
-        best = pmine[src]
-        for c in copies:
-            c.wait_recv()
-        first = {1: 0, 2: 1, 3: 6}[dst]
-        for j in range(len(copies)):
-            best = jnp.maximum(best, pbuf[first + j])
-        pmine[dst] = best
-
-    pl.semaphore_wait(barrier, len(peers))
-    for c in p_first:
-        c.start()
+    to_root = lambda: pltpu.make_async_remote_copy(
+        src_ref=pmine.at[0], dst_ref=pbuf.at[z], send_sem=sp.at[0], recv_sem=rp.at[z],
+        device_id={"gx": at(yh, 0), "head": hd}, device_id_type=MESH,
+    )
+    to_other = lambda: pltpu.make_async_remote_copy(
+        src_ref=pmine.at[0], dst_ref=pbuf.at[Z + z], send_sem=sp.at[1], recv_sem=rp.at[Z + z],
+        device_id={"gx": at(1 - yh, 0), "head": across}, device_id_type=MESH,
+    )
+    answer = lambda i: pltpu.make_async_remote_copy(
+        src_ref=pmine.at[1], dst_ref=pbuf.at[2 * Z], send_sem=sp.at[1 + i], recv_sem=rp.at[2 * Z],
+        device_id={"gx": at(yh, i), "head": hd}, device_id_type=MESH,
+    )
+    arrived = lambda slot: pltpu.make_async_remote_copy(
+        src_ref=pmine.at[0], dst_ref=pbuf.at[slot], send_sem=sp.at[0], recv_sem=rp.at[slot],
+        device_id={"gx": at(1 - yh, 0), "head": across}, device_id_type=MESH,
+    )
+
+    greeters = 3 + (g > 0).astype(jnp.int32) + (g < ng - 1).astype(jnp.int32) + (z > 0).astype(jnp.int32)
+    pl.semaphore_wait(barrier, greeters)
+
+    @pl.when(z > 0)
+    def _():
+        to_root().start()
+
+    to_other().start()
     send_x(0, True)
     send_x(0, False)
     for chunk in range(3):
         send_h(0, chunk)
 
+    for i in range(NXL):
+        wx[i] = jnp.broadcast_to(wv[i, 0:1, :], (NV, NY))
+        wy[i] = jnp.broadcast_to(wv[i, 1:2, :], (NV, NY))
     get_mask.wait()
     get_depth.wait()
     for i in range(NXL):
@@ -321,17 +333,10 @@
     get_tab.wait()
     get_level.wait()
 
-    pass_vy(u0, r, wy, tab, by, None, 0, 3)
-    fold(p_first, 0, 1)
-    for c in p_near:
-        c.start()
-    pass_vy(u0, r, wy, tab, by, None, 3, NXL)
+    pass_vy(u0, r, wy, tab, by, None, 0, NXL)
     for chunk in range(3):
         take_h(0, chunk)
     pass_h(u0, r, 0, NXL)
-    fold(p_near, 1, 2)
-    for c in p_far:
-        c.start()
 
     def keep(x, h, part, jump):
         r[x, h] = r[x, h] + part
@@ -343,8 +348,22 @@
     take_x(0, False)
     pass_x(u0, wx, tab, 6, keep)
 
-    fold(p_far, 2, 3)
-    top = pmine[3]
+    @pl.when(z == 0)
+    def _():
+        best = pmine[0]
+        for slot in range(1, 2 * Z):
+            arrived(slot).wait_recv()
+            best = jnp.maximum(best, pbuf[slot])
+        pmine[1] = best
+        for i in range(1, Z):
+            answer(i).start()
+
+    @pl.when(z > 0)
+    def _():
+        arrived(2 * Z).wait_recv()
+        pmine[1] = pbuf[2 * Z]
+
+    top = pmine[1]
     cx, cnx, cy, cny = bounds()
     peak_x = jnp.maximum(top[0:1] + cx, top[1:2] + cnx)
     peak_y = jnp.maximum(top[2:3] + cy, top[3:4] + cny)
@@ -414,8 +433,18 @@
 
     for put in puts:
         put.wait()
-    for c in p_first + p_near + p_far:
-        c.wait_send()
+
+    @pl.when(z > 0)
+    def _():
+        to_root().wait_send()
+
+    to_other().wait_send()
+
+    @pl.when(z == 0)
+    def _():
+        for i in range(1, Z):
+            answer(i).wait_send()
+
     for s in range(3):
         for up in (True, False):
 
@@ -439,19 +468,19 @@
         out_specs=pl.BlockSpec(memory_space=pl.ANY),
         scratch_shapes=[
             field, field, field, inner, inner, inner, inner,
-            pltpu.VMEM((2, NXL, NY), jnp.float32),
+            pltpu.VMEM((NXL, 2, NY), jnp.float32),
             pltpu.VMEM((NXL, NY), jnp.int32),
             pltpu.VMEM((NXL, NY), jnp.float32),
             pltpu.VMEM((2 * NHL, NY), jnp.float32),
             rows, rows, rows,
             pltpu.VMEM((3, NV, NY), jnp.float32),
-            pltpu.VMEM((8, NV, NY), jnp.float32),
-            pltpu.VMEM((4, NV, NY), jnp.float32),
-            dma((5,)), dma((3, 2)), dma((3, 2)), dma((3, 2, 3)), dma((3, 2, 3)), dma((8,)), dma((8,)), dma((3,)),
+            pltpu.VMEM((2 * Z + 1, NV, NY), jnp.float32),
+            pltpu.VMEM((2, NV, NY), jnp.float32),
+            dma((5,)), dma((3, 2)), dma((3, 2)), dma((3, 2, 3)), dma((3, 2, 3)), dma((Z + 1,)), dma((2 * Z + 1,)), dma((3,)),
         ],
         compiler_params=pltpu.CompilerParams(collective_id=0, has_side_effects=True),
         name="step",
-    )(level_set, wind_field, target_mask, target_depth, jnp.asarray(table()))
+    )(level_set, jnp.transpose(wind_field, (1, 0, 2)), target_mask, target_depth, jnp.asarray(table()))
 
 
 def solution(mesh):

time: 43.4 us -> 39.7 us (0.915)
  Pallas kernels: 40.1 us -> 37.7 us
  local copies, waits for them, and re-layouts: 3.11 us -> 1.8 us
    pallas_call x1, Pallas kernels: 40.1 us -> 37.7 us  [local(): pl.pallas_call(kernel, out_shape=jax.ShapeDtypeStruct(level_set.shape, jn...]
    unnamed x2 -> x1, local copies, waits for them, and re-layouts: 3.11 us -> 1.8 us
where the time goes in v2:
time: 39.7 us; the launch traced here: 39.5 us
  Pallas kernels  37.7 us (95%)
  local copies, waits for them, and re-layouts  1.8 us (5%)
    pallas_call x1, Pallas kernels, local(): pl.pallas_call(kernel, out_shape=jax.ShapeDtypeStruct(level_set.shape, jn...  37.7 us
    unnamed x1, local copies, waits for them, and re-layouts  1.8 us

profile of v2, /device:TPU:16, one launch (start us, length us, event | category | flops | bytes accessed | tf_op | source)
XLA Modules:
  0.0 39.5 jit_solution(6352220940430119036)
XLA Ops:
  0.0 37.7 %step.1 = f32[9,12,8,128]{3,2,1,0:T(8,128)} custom-call(f32[9,12,8,128]{3,2,1,0:T(8,128)} %level.1, f32[9,2,128]{2,1,0:T(2,128)} %bitcast.1, s32[9,128]{1,0:T(8,128)} %mask.1, f32[9,128]{1,0:T(8,128)} %depth.1, f32[16,24,128]{2,1,0:T(8,128)} %constant.2.clone.tab_all), custom_call_target="tpu_custom_call" | custom-call | tf_op jit(solution)/shard_map/step/pallas_call | solution.py:464
  37.7 1.8 %copy.7 = f32[9,12,8,128]{3,2,1,0:T(8,128)} copy(f32[9,12,8,128]{3,2,1,0:T(8,128)} %step.1) | data formatting | bytes 884736

commit v3 on v2

--- a/solution.py
+++ b/solution.py
@@ -194,6 +194,9 @@
     across = (hd + nh // 2) % nh
     fields = (u0, u1, u2)
 
+    get_wind = pltpu.make_async_copy(wind, wv, sem_in.at[0])
+    get_wind.start()
+
     barrier = pltpu.get_barrier_semaphore()
 
     def greet(peer):
@@ -217,8 +220,6 @@
         for i in range(Z):
             greet({"gx": at(1 - yh, i), "head": across})
 
-    get_wind = pltpu.make_async_copy(wind, wv, sem_in.at[0])
-    get_wind.start()
     get_level = pltpu.make_async_copy(level, u0.at[pl.ds(3, NXL), pl.ds(3, NHL)], sem_in.at[1])
     get_level.start()
     get_tab = pltpu.make_async_copy(tab_all.at[hd], tab, sem_in.at[2])
@@ -342,11 +343,26 @@
         r[x, h] = r[x, h] + part
         bx[x, h] = jump
 
+    def either(low, first, second):
+        pl.when(low)(first)
+        pl.when(jnp.logical_not(low))(second)
+
+    def both_sides(s, finish, after):
+        for low in (g != Z, g == Z):
+
+            @pl.when(low)
+            def _():
+                take_x(s, True)
+
+            @pl.when(jnp.logical_not(low))
+            def _():
+                take_x(s, False)
+
+            pass_x(fields[s], wx, tab, jnp.where(low, 0, 6), finish)
+            after(low)
+
     pass_x(u0, wx, tab, 3, keep)
-    take_x(0, True)
-    pass_x(u0, wx, tab, 0, keep)
-    take_x(0, False)
-    pass_x(u0, wx, tab, 6, keep)
+    both_sides(0, keep, lambda low: None)
 
     @pl.when(z == 0)
     def _():
@@ -406,12 +422,7 @@
 
         pass_x(u, wx, tab, 3, finish)
         after(1)
-        take_x(s, True)
-        pass_x(u, wx, tab, 0, finish)
-        after(0)
-        take_x(s, False)
-        pass_x(u, wx, tab, 6, finish)
-        after(2)
+        both_sides(s, finish, lambda low: either(low, lambda: after(0), lambda: after(2)))
 
     def write_two(x, h, value):
         u2[x + 3, h + 3] = value
@@ -461,10 +472,11 @@
     inner = pltpu.VMEM((NXL, NHL, NV, NY), jnp.float32)
     rows = pltpu.VMEM((NXL, NV, NY), jnp.float32)
     dma = pltpu.SemaphoreType.DMA
+    inputs = (level_set, jnp.transpose(wind_field, (1, 0, 2)), target_mask, target_depth, jnp.asarray(table()))
     return pl.pallas_call(
         kernel,
         out_shape=jax.ShapeDtypeStruct(level_set.shape, jnp.float32),
-        in_specs=[pl.BlockSpec(memory_space=pl.ANY)] * 5,
+        in_specs=[pl.BlockSpec(memory_space=pltpu.HBM)] * 5,
         out_specs=pl.BlockSpec(memory_space=pl.ANY),
         scratch_shapes=[
             field, field, field, inner, inner, inner, inner,
@@ -478,9 +490,9 @@
             pltpu.VMEM((2, NV, NY), jnp.float32),
             dma((5,)), dma((3, 2)), dma((3, 2)), dma((3, 2, 3)), dma((3, 2, 3)), dma((Z + 1,)), dma((2 * Z + 1,)), dma((3,)),
         ],
-        compiler_params=pltpu.CompilerParams(collective_id=0, has_side_effects=True),
+        compiler_params=pltpu.CompilerParams(collective_id=0, has_side_effects=True, vmem_limit_bytes=32 * 1024 * 1024),
         name="step",
-    )(level_set, jnp.transpose(wind_field, (1, 0, 2)), target_mask, target_depth, jnp.asarray(table()))
+    )(*[pltpu.with_memory_space_constraint(a, pltpu.HBM) for a in inputs])
 
 
 def solution(mesh):

time: 39.7 us -> 38.2 us (0.962)
  local copies, waits for them, and re-layouts: 1.8 us -> 0.76 us
  Pallas kernels: 37.7 us -> 37.3 us
    unnamed x1, local copies, waits for them, and re-layouts: 1.8 us -> 0.76 us
where the time goes in v3:
time: 38.2 us; the launch traced here: 38.1 us
  Pallas kernels  37.3 us (98%)
  local copies, waits for them, and re-layouts  0.76 us (2%)
    pallas_call x1, Pallas kernels, local(): pl.pallas_call(kernel, out_shape=jax.ShapeDtypeStruct(level_set.shape, jn...  37.3 us
    unnamed x1, local copies, waits for them, and re-layouts  0.76 us

profile of v3, /device:TPU:16, one launch (start us, length us, event | category | flops | bytes accessed | tf_op | source)
XLA Modules:
  0.0 38.1 jit_solution(6652028994341033760)
XLA Ops:
  0.0 37.3 %step.1 = f32[9,12,8,128]{3,2,1,0:T(8,128)S(1)} custom-call(f32[9,12,8,128]{3,2,1,0:T(8,128)} %level.1, f32[9,2,128]{2,1,0:T(2,128)} %bitcast.1, s32[9,128]{1,0:T(8,128)} %mask.1, f32[9,128]{1,0:T(8,128)} %depth.1, f32[16,24,128]{2,1,0:T(8,128)} %constant.2.clone.tab_all), custom_call_target="tpu_custom_call" | custom-call | tf_op jit(solution)/shard_map/step/pallas_call | solution.py:476
  37.3 0.8 %copy.7 = f32[9,12,8,128]{3,2,1,0:T(8,128)} copy(f32[9,12,8,128]{3,2,1,0:T(8,128)S(1)} %step.1) | data formatting | bytes 884736
